TPU v7x, 256 devices: a whole 4x4x8 slice. The times are simulated.
256 devices in a mesh: dp: 2 (over core), row: 16 (over y, x), col: 8 (over z).
Axes of the slice: x: 4, y: 4, z: 8, core: 2. Of those that a mesh axis runs over, the one named last changes fastest.
Arguments:
- features: bfloat16 [2, 256, 128, 1024], P('dp', None, 'row', 'col'), may hold values from -41 to 41, as said below
- group_kernel: bfloat16 [256, 72], replicated, may hold values from -0.75 to 0.75
- norm_gain: float32 [256], replicated, may hold values from 0.1 to 1.9
- norm_bias: float32 [256], replicated, may hold values from -3 to 3
- mix_weight: bfloat16 [256, 256], replicated, may hold values from -0.375 to 0.375
- cotangent: bfloat16 [2, 256, 128, 1024], P('dp', None, 'row', 'col'), may hold values from -6 to 6
Outputs:
- mixed: bfloat16 [2, 256, 128, 1024], P('dp', None, 'row', 'col')
- grad_features: bfloat16 [2, 256, 128, 1024], P('dp', None, 'row', 'col')
- grad_mix: float32 [256, 256], replicated
- grad_gain: float32 [256], replicated
- grad_bias: float32 [256], replicated
- grad_kernel: float32 [256, 72], replicated
- grad_whiten: float32 [2, 256, 256], P('dp')
Inputs may be any that keep to these rules, and one draw needn't show every extreme that they name: `features`: feature maps whose scale varies over channels and over cells.
All inputs are finite; a program needn't handle non-finite values.
Results may differ from a plain program's by a relative error of at most 0.0085.
Values may be sent and summed in bfloat16 or wider, within the bound.
A program may use at most 64 MiB of HBM per device.

v0:
```python
import jax
import jax.numpy as jnp
from jax import lax
from jax.sharding import PartitionSpec as P

GROUPS = 32
NEWTON = 5
EPS = 1e-05


def with_halo(block, sides, width):
    for axis, dim in sides:
        count = lax.axis_size(axis)
        forward = [(i, i + 1) for i in range(count - 1)]
        backward = [(target, source) for source, target in forward]
        low = lax.ppermute(
            lax.slice_in_dim(block, block.shape[dim] - width, None, axis=dim), axis, forward
        )
        high = lax.ppermute(lax.slice_in_dim(block, 0, width, axis=dim), axis, backward)
        block = jnp.concatenate([low, block, high], axis=dim)
    return block


def group_conv(padded, kernel):
    chans, prow, pcol = padded.shape
    height = prow - 2
    width = pcol - 2
    gwidth = chans // GROUPS
    pieces = padded.reshape(GROUPS, gwidth, prow, pcol)
    weights = kernel.reshape(GROUPS, gwidth, gwidth, 9)
    total = jnp.zeros((GROUPS, gwidth, height, width), jnp.float32)
    for position in range(9):
        shift_row, shift_col = divmod(position, 3)
        window = pieces[:, :, shift_row : shift_row + height, shift_col : shift_col + width]
        total = total + jnp.einsum(
            "goi,girw->gorw", weights[..., position], window, preferred_element_type=jnp.float32
        )
    return total.reshape(chans, height, width)


def conv_transpose(grad_pad, kernel):
    chans, prow, pcol = grad_pad.shape
    height = prow - 2
    width = pcol - 2
    gwidth = chans // GROUPS
    pieces = grad_pad.reshape(GROUPS, gwidth, prow, pcol)
    weights = kernel.reshape(GROUPS, gwidth, gwidth, 9)
    total = jnp.zeros((GROUPS, gwidth, height, width), jnp.float32)
    for position in range(9):
        shift_row, shift_col = divmod(position, 3)
        window = pieces[
            :, :, 2 - shift_row : 2 - shift_row + height, 2 - shift_col : 2 - shift_col + width
        ]
        total = total + jnp.einsum(
            "goi,gorw->girw", weights[..., position], window, preferred_element_type=jnp.float32
        )
    return total.reshape(chans, height, width)


def kernel_grad(grad_conv, padded):
    chans, height, width = grad_conv.shape
    gwidth = chans // GROUPS
    grads = grad_conv.reshape(GROUPS, gwidth, height, width)
    pieces = padded.reshape(GROUPS, gwidth, height + 2, width + 2)
    parts = []
    for position in range(9):
        shift_row, shift_col = divmod(position, 3)
        window = pieces[:, :, shift_row : shift_row + height, shift_col : shift_col + width]
        parts.append(
            jnp.einsum("gorw,girw->goi", grads, window, preferred_element_type=jnp.float32)
        )
    return jnp.stack(parts, axis=-1).reshape(chans, gwidth * 9)


def whitening(covariance):
    trace_value = jnp.trace(covariance)
    normed = covariance / trace_value
    proj = jnp.eye(covariance.shape[0], dtype=jnp.float32)
    for step in range(NEWTON):
        cube = jnp.dot(
            jnp.dot(proj, proj, precision=lax.Precision.HIGHEST),
            proj,
            precision=lax.Precision.HIGHEST,
        )
        proj = 0.5 * (3.0 * proj - jnp.dot(cube, normed, precision=lax.Precision.HIGHEST))
    return proj / jnp.sqrt(trace_value)


def local(features, group_kernel, norm_gain, norm_bias, mix_weight, cotangent):
    image = features[0]
    chans, height, width = image.shape
    local_cells = height * width
    cells = height * lax.axis_size("row") * width * lax.axis_size("col")
    scenes = features.shape[0] * lax.axis_size("dp")
    eye_mat = jnp.eye(chans, dtype=jnp.float32)
    padded = with_halo(image, (("row", 1), ("col", 2)), 1)
    conv = group_conv(padded, group_kernel).astype(jnp.bfloat16)
    flat = conv.reshape(chans, local_cells)
    channel_mean = lax.psum(jnp.sum(flat, axis=1, dtype=jnp.float32), ("row", "col")) / cells
    centered = flat.astype(jnp.float32) - channel_mean[:, None]
    moments = jnp.dot(centered, centered.T, precision=lax.Precision.HIGHEST)
    covariance = lax.psum(moments, ("row", "col")) / cells + EPS * eye_mat
    whiten = whitening(covariance)
    normed = jnp.dot(whiten, centered, precision=lax.Precision.HIGHEST)
    shifted = norm_gain[:, None] * normed + norm_bias[:, None]
    gate = jax.nn.sigmoid(shifted)
    act = (shifted * gate).astype(jnp.bfloat16)
    mixed = (
        image.reshape(chans, local_cells).astype(jnp.float32)
        + jnp.dot(mix_weight, act, preferred_element_type=jnp.float32)
    ).astype(jnp.bfloat16)
    upstream = cotangent[0].reshape(chans, local_cells)
    dact = jnp.dot(mix_weight.T, upstream, preferred_element_type=jnp.float32)
    dshift = dact * gate * (1.0 + shifted * (1.0 - gate))
    mix_part = jnp.dot(upstream, act.T, preferred_element_type=jnp.float32)
    gain_part = jnp.sum(dshift * normed, axis=1)
    bias_part = jnp.sum(dshift, axis=1)
    dnormed = (norm_gain[:, None] * dshift).astype(jnp.bfloat16)
    white_part = jnp.dot(dnormed, flat.T, preferred_element_type=jnp.float32)
    sum_part = jnp.sum(dnormed, axis=1, dtype=jnp.float32)
    white_total, grad_sum = lax.psum((white_part, sum_part), ("row", "col"))
    dwhiten = white_total - jnp.outer(grad_sum, channel_mean)
    white_out = (dwhiten / jnp.sqrt(jnp.float32(cells)))[None]
    unused, pullback = jax.vjp(whitening, covariance)
    dcov = pullback(dwhiten)[0]
    dsym = 0.5 * (dcov + dcov.T)
    left_side = jnp.concatenate([whiten.T, dsym * (2.0 / cells)], axis=1)
    right_side = jnp.concatenate(
        [dnormed.astype(jnp.float32) - (grad_sum / cells)[:, None], centered], axis=0
    )
    dconv = jnp.dot(left_side, right_side, precision=lax.Precision.HIGHEST).astype(jnp.bfloat16)
    dconv = dconv.reshape(chans, height, width)
    grad_pad = with_halo(dconv, (("row", 1), ("col", 2)), 1)
    grad_image = (cotangent[0].astype(jnp.float32) + conv_transpose(grad_pad, group_kernel)).astype(
        jnp.bfloat16
    )
    kernel_part = kernel_grad(dconv, padded)
    scale = 1.0 / jnp.sqrt(jnp.float32(scenes * cells))
    grad_mix, grad_gain, grad_bias, grad_kernel = lax.psum(
        (mix_part, gain_part, bias_part, kernel_part), ("dp", "row", "col")
    )
    return (
        mixed.reshape(features.shape),
        grad_image.reshape(features.shape),
        grad_mix * scale,
        grad_gain * scale,
        grad_bias * scale,
        grad_kernel * scale,
        white_out,
    )


def solution(mesh):
    in_specs = (P("dp", None, "row", "col"), P(), P(), P(), P(), P("dp", None, "row", "col"))
    out_specs = (
        P("dp", None, "row", "col"),
        P("dp", None, "row", "col"),
        P(),
        P(),
        P(),
        P(),
        P("dp", None, None),
    )
    return jax.shard_map(local, mesh=mesh, in_specs=in_specs, out_specs=out_specs, check_vma=False)
```

profile of v0, /device:TPU:1, one launch (start us, length us, event | category | flops | bytes accessed | tf_op | source)
XLA Modules:
  0.0 1363.5 jit_solution(14939398661312466481)
XLA Ops:
  8.4 3.9 collective-permute-start
  12.3 1.3 collective-permute-start.1
  15.0 2.3 collective-permute-done.1
  18.1 3.5 collective-permute-start.2
  22.0 1.3 collective-permute-start.3
  23.3 1.4 copy.199
  27.8 1.2 fusion.222
  32.4 296.3 %psum.56 = f32[256]{0:T(256)S(1)} all-reduce(f32[256]{0:T(256)S(1)} %reduce_sum.72), channel_id=1, replica_groups=mesh['dp'=2,'row'=16,'col'=8] {'row','col'}, use_global_device_ids=true, to_apply=%region_1.0 | all-reduce | flops 256 | bytes 2048 | tf_op jit(solution)/shard_map/psum | solution.py:99
  328.7 1.9 fusion.24
  331.4 258.6 %all-reduce.6.cloned.1.call-done = f32[256,256]{1,0:T(8,128)} async-done(((f32[256,256]{1,0:T(8,128)}), f32[256,256]{1,0:T(8,128)}) %all-reduce.6.cloned.1.call-update) | async-done | bytes 262160 | tf_op jit(solution)/shard_map/psum | solution.py:102
  599.1 1.7 fusion.217
  603.6 1.7 fusion.216
  608.2 2.9 fusion.79
  612.2 1.2 fusion.84
  613.5 2.1 fusion.220
  617.5 291.8 %psum.59 = f32[256]{0:T(256)S(1)} all-reduce(f32[256]{0:T(256)S(1)} %get-tuple-element.62), channel_id=1, replica_groups=mesh['dp'=2,'row'=16,'col'=8] {'row','col'}, use_global_device_ids=true, to_apply=%region_6.7 | all-reduce | flops 256 | bytes 2048 | tf_op jit(solution)/shard_map/psum | solution.py:121
  909.5 2.3 convolution_bitcast_fusion.1
  912.9 2.1 copy.273
  915.0 131.0 %all-reduce = (f32[256]{0:T(256)S(1)}, f32[256]{0:T(256)S(1)}) all-reduce(f32[256]{0:T(256)} %get-tuple-element.36, f32[256]{0:T(256)S(1)} %get-tuple-element.35), channel_id=1, replica_groups=mesh['dp'=2,'row'=16,'col'=8] {'dp','row','col'}, use_global_device_ids=true, to_apply=%region_11.12 | all-reduce | flops 512 | bytes 4096 | tf_op jit(solution)/shard_map/psum | solution.py:139
  1047.8 2.3 fusion.90
  1060.9 1.3 convolution_add_fusion.19
  1062.3 1.5 multiply_bitcast_fusion
  1064.4 1.6 convolution_add_fusion.18
  1069.4 1.8 multiply_reduce_fusion.1
  1072.1 2.9 fusion.8
  1079.0 3.2 collective-permute-start.4
  1082.6 1.3 collective-permute-start.5
  1084.1 3.6 collective-permute-done.5
  1088.3 3.7 collective-permute-start.6
  1092.4 1.5 collective-permute-start.7
  1095.0 2.9 copy.272
  1111.4 241.7 %all-reduce.10.cloned.1.call-done = (f32[256,256]{0,1:T(8,128)}, f32[256,72]{1,0:T(8,128)}) async-done(((f32[256,256]{0,1:T(8,128)}, f32[256,72]{1,0:T(8,128)}), (f32[256,256]{0,1:T(8,128)}, f32[256,72]{1,0:T(8,128)})) %all-reduce.10.cloned.1.call-update) | async-done | bytes 335888 | tf_op jit(solution)/shard_map/psum | solution.py:139
  (295 shorter events, 66.9 us)
Async XLA Ops:
  7.2 606.3 %copy-start = (bf16[256,256]{1,0:T(8,128)(2,1)S(1)}, bf16[256,256]{1,0:T(8,128)(2,1)}, u32[]{:S(2)}) copy-start(bf16[256,256]{1,0:T(8,128)(2,1)} %param.10) | copy-start | bytes 393220
  7.2 6.7 copy-start.76
  7.2 582.8 %all-reduce.6.cloned.1.call-start = ((), (), s32[]{:S(2)}) async-start(), calls=%async_computation | async-start | bytes 524288 | tf_op jit(solution)/shard_map/psum | solution.py:102
  8.4 6.6 collective-permute-start
  12.3 5.0 collective-permute-start.1
  15.0 578.5 %copy-start.51 = (f32[256,256]{1,0:T(8,128)}, f32[256,256]{1,0:T(8,128)S(1)}, u32[]{:S(2)}) copy-start(f32[256,256]{1,0:T(8,128)S(1)} %fusion.88) | copy-start | bytes 786436
  17.7 5.6 copy-start.20
  18.1 8.2 collective-permute-start.2
  22.0 4.7 collective-permute-start.3
  24.9 4.2 copy-start.53
  25.0 4.4 copy-start.69
  25.2 4.6 copy-start.67
  25.3 5.0 copy-start.65
  25.5 5.1 copy-start.63
  25.7 5.3 copy-start.61
  25.8 5.4 copy-start.59
  26.0 5.6 copy-start.57
  26.1 5.8 copy-start.55
  330.7 717.2 %all-reduce.8.cloned.1.call-start = ((), (), s32[]{:S(2)}) async-start(), calls=%async_computation.1 | async-start | bytes 524288 | tf_op jit(solution)/shard_map/psum | solution.py:121
  590.9 17.2 %copy-start.3 = (f32[256,256]{1,0:T(8,128)}, f32[256,256]{1,0:T(8,128)S(1)}, u32[]{:S(2)}) copy-start(f32[256,256]{1,0:T(8,128)S(1)} %multiply_add_fusion.1) | copy-start | bytes 786436
  598.7 3.2 copy-start.8
  617.4 294.3 %copy-start.2 = (f32[1,256,8,128]{1,3,2,0:T(8,128)S(1)}, f32[1,256,8,128]{1,3,2,0:T(8,128)}, u32[]{:S(2)}) copy-start(f32[1,256,8,128]{1,3,2,0:T(8,128)} %copy.199) | copy-start | bytes 3145732
  617.5 735.6 %all-reduce.10.cloned.1.call-start = ((), (), s32[]{:S(2)}) async-start(), calls=%async_computation.2 | async-start | bytes 786432 | tf_op jit(solution)/shard_map/psum | solution.py:139
  1078.2 4.1 copy-start.25
  1079.0 4.9 collective-permute-start.4
  1082.6 5.0 copy-start.41
  1082.6 5.0 collective-permute-start.5
  1087.9 6.0 copy-start.23
  1088.3 11.3 collective-permute-start.6
  1092.4 7.7 collective-permute-start.7
  1095.0 3.8 copy-start.42
  1109.7 246.9 %copy-start.1 = (bf16[256,256]{1,0:T(8,128)(2,1)S(1)}, bf16[256,256]{1,0:T(8,128)(2,1)}, u32[]{:S(2)}) copy-start(bf16[256,256]{1,0:T(8,128)(2,1)} %param.10) | copy-start | bytes 393220
  (58 other events, 90.8 us)
Sparse Core Ops, SparseCore 0:
  330.8 259.1 all-reduce.5
  617.6 213.4 all-reduce.7
  1099.8 253.2 all-reduce.9
where the time goes:
time: 1370 us; the launch traced here: 1360 us
  blocking collectives  719 us (52%)
  waiting for transfers between devices  506 us (37%)
  matrix products  55.7 us (4%)
  local copies, waits for them, and re-layouts  33.5 us (2%)
  starting transfers between devices  20.5 us (1%)
  between operations  19 us (1%)
    psum x1, blocking collectives, local(): lax.psum(jnp.sum(flat, axis=1, dtype=jnp.float32), ('row', 'col')) / cells  296 us
    psum x1, blocking collectives, local(): white_total, grad_sum = lax.psum((white_part, sum_part), ('row', 'col'))  292 us
    psum x1, waiting for transfers between devices, local(): covariance = lax.psum(moments, ('row', 'col')) / cells + EPS * eye_mat  259 us
    psum x1, waiting for transfers between devices, local(): lax.psum((mix_part, gain_part, bias_part, kernel_part), ('dp', 'row', 'co...  242 us
    psum x1, blocking collectives, local(): lax.psum((mix_part, gain_part, bias_part, kernel_part), ('dp', 'row', 'co...  131 us
  transfers between devices with their start and end apart: 11, of which 4 were waited for; matrix products, arithmetic and copies ran while one was open for 2% of the time, Pallas kernels for 0%

commit v1 on v0

--- a/solution.py
+++ b/solution.py
@@ -99,7 +99,7 @@
     channel_mean = lax.psum(jnp.sum(flat, axis=1, dtype=jnp.float32), ("row", "col")) / cells
     centered = flat.astype(jnp.float32) - channel_mean[:, None]
     moments = jnp.dot(centered, centered.T, precision=lax.Precision.HIGHEST)
-    covariance = lax.psum(moments, ("row", "col")) / cells + EPS * eye_mat
+    covariance = lax.psum(lax.psum(moments, "col"), "row") / cells + EPS * eye_mat
     whiten = whitening(covariance)
     normed = jnp.dot(whiten, centered, precision=lax.Precision.HIGHEST)
     shifted = norm_gain[:, None] * normed + norm_bias[:, None]

time: 1370 us -> 1320 us (0.964)
  waiting for transfers between devices: 506 us -> 462 us
    psum x1 -> x2, waiting for transfers between devices: 259 us -> 213 us  [the longest x1 114 us: local(): lax.psum(moments, 'col')]
  transfers between devices with their start and end apart: 11 -> 12, of which waited for: 4 -> 6; matrix products, arithmetic and copies ran while one was open for 2% -> 2% of each run, Pallas kernels for 0% -> 0%
where the time goes in v1:
time: 1320 us
  blocking collectives  716 us (54%)
  waiting for transfers between devices  462 us (35%)
  matrix products  53.5 us (4%)
  local copies, waits for them, and re-layouts  34.9 us (3%)
  starting transfers between devices  20.5 us (2%)
  between operations  19 us (1%)
    psum x1, blocking collectives, local(): lax.psum(jnp.sum(flat, axis=1, dtype=jnp.float32), ('row', 'col')) / cells  295 us
    psum x1, blocking collectives, local(): white_total, grad_sum = lax.psum((white_part, sum_part), ('row', 'col'))  293 us
    psum x1, waiting for transfers between devices, local(): lax.psum((mix_part, gain_part, bias_part, kernel_part), ('dp', 'row', 'co...  242 us
    psum x1, blocking collectives, local(): lax.psum((mix_part, gain_part, bias_part, kernel_part), ('dp', 'row', 'co...  128 us
    psum x1, waiting for transfers between devices, local(): lax.psum(moments, 'col')  114 us
    psum x1, waiting for transfers between devices, local(): lax.psum(lax.psum(moments, 'col'), 'row') / cells + EPS * eye_mat  99.1 us
  transfers between devices with their start and end apart: 12, of which 6 were waited for; matrix products, arithmetic and copies ran while one was open for 2% of the time, Pallas kernels for 0%

profile of v1, /device:TPU:1, one launch (start us, length us, event | category | flops | bytes accessed | tf_op | source)
XLA Modules:
  0.0 1316.3 jit_solution(576588908860825181)
XLA Ops:
  8.4 3.9 collective-permute-start
  12.3 1.3 collective-permute-start.1
  14.4 2.9 collective-permute-done.1
  18.1 3.5 collective-permute-start.2
  22.0 1.3 collective-permute-start.3
  25.2 1.4 collective-permute-done.3
  32.3 294.8 %psum.63 = f32[256]{0:T(256)S(1)} all-reduce(f32[256]{0:T(256)S(1)} %reduce_sum.72), channel_id=1, replica_groups=mesh['dp'=2,'row'=16,'col'=8] {'row','col'}, use_global_device_ids=true, to_apply=%region_1.0 | all-reduce | flops 256 | bytes 2048 | tf_op jit(solution)/shard_map/psum | solution.py:99
  327.2 1.9 fusion.24
  329.4 1.4 copy.199
  331.3 113.5 %all-reduce.7.cloned.1.call-done = f32[256,256]{1,0:T(8,128)} async-done(((f32[256,256]{1,0:T(8,128)}), f32[256,256]{1,0:T(8,128)}) %all-reduce.7.cloned.1.call-update) | async-done | bytes 262160 | tf_op jit(solution)/shard_map/psum | solution.py:102
  445.5 99.1 %all-reduce.9.cloned.1.call-done = f32[256,256]{1,0:T(8,128)} async-done(((f32[256,256]{1,0:T(8,128)}), f32[256,256]{1,0:T(8,128)}) %all-reduce.9.cloned.1.call-update) | async-done | bytes 262160 | tf_op jit(solution)/shard_map/psum | solution.py:102
  558.1 1.7 fusion.216
  559.8 1.8 copy.230
  564.3 2.9 fusion.79
  568.4 1.2 fusion.84
  569.6 2.1 fusion.220
  573.7 292.5 %psum.67 = f32[256]{0:T(256)S(1)} all-reduce(f32[256]{0:T(256)S(1)} %get-tuple-element.62), channel_id=1, replica_groups=mesh['dp'=2,'row'=16,'col'=8] {'row','col'}, use_global_device_ids=true, to_apply=%region_7.8 | all-reduce | flops 256 | bytes 2048 | tf_op jit(solution)/shard_map/psum | solution.py:121
  866.3 2.2 convolution_bitcast_fusion.1
  868.6 2.4 fusion.11
  871.0 2.2 copy.273
  873.1 128.3 %all-reduce = (f32[256]{0:T(256)S(1)}, f32[256]{0:T(256)S(1)}) all-reduce(f32[256]{0:T(256)} %get-tuple-element.36, f32[256]{0:T(256)S(1)} %get-tuple-element.35), channel_id=1, replica_groups=mesh['dp'=2,'row'=16,'col'=8] {'dp','row','col'}, use_global_device_ids=true, to_apply=%region_12.13 | all-reduce | flops 512 | bytes 4096 | tf_op jit(solution)/shard_map/psum | solution.py:139
  1003.2 2.2 fusion.90
  1016.7 1.5 multiply_bitcast_fusion
  1023.0 1.9 multiply_reduce_fusion.1
  1025.8 1.9 fusion.8
  1031.7 3.2 collective-permute-start.4
  1035.3 1.3 collective-permute-start.5
  1036.8 3.6 collective-permute-done.5
  1041.0 3.7 collective-permute-start.6
  1045.1 1.5 collective-permute-start.7
  1047.7 2.9 copy.272
  1064.1 241.8 %all-reduce.13.cloned.1.call-done = (f32[256,256]{0,1:T(8,128)}, f32[256,72]{1,0:T(8,128)}) async-done(((f32[256,256]{0,1:T(8,128)}, f32[256,72]{1,0:T(8,128)}), (f32[256,256]{0,1:T(8,128)}, f32[256,72]{1,0:T(8,128)})) %all-reduce.13.cloned.1.call-update) | async-done | bytes 335888 | tf_op jit(solution)/shard_map/psum | solution.py:139
  (292 shorter events, 69.5 us)
Async XLA Ops:
  7.2 562.4 %copy-start = (bf16[256,256]{1,0:T(8,128)(2,1)S(1)}, bf16[256,256]{1,0:T(8,128)(2,1)}, u32[]{:S(2)}) copy-start(bf16[256,256]{1,0:T(8,128)(2,1)} %param.10) | copy-start | bytes 393220
  7.2 6.4 copy-start.73
  7.2 437.6 %all-reduce.7.cloned.1.call-start = ((), (), s32[]{:S(2)}) async-start(), calls=%async_computation | async-start | bytes 524288 | tf_op jit(solution)/shard_map/psum | solution.py:102
  8.4 6.0 collective-permute-start
  12.3 5.0 collective-permute-start.1
  18.1 6.7 collective-permute-start.2
  22.0 4.6 collective-permute-start.3
  23.5 5.5 copy-start.47
  23.6 5.7 copy-start.63
  23.8 5.9 copy-start.61
  24.0 6.3 copy-start.59
  24.1 6.4 copy-start.57
  24.3 6.6 copy-start.55
  24.4 6.7 copy-start.53
  24.6 6.9 copy-start.51
  24.8 7.0 copy-start.49
  32.2 297.2 %copy-start.13 = (bf16[1,256,8,128]{3,2,1,0:T(8,128)(2,1)S(1)}, bf16[1,256,8,128]{3,2,1,0:T(8,128)(2,1)}, u32[]{:S(2)}) copy-start(bf16[1,256,8,128]{3,2,1,0:T(8,128)(2,1)} %param.6) | copy-start | bytes 1572868
  329.1 215.5 %all-reduce.9.cloned.1.call-start = ((), (), s32[]{:S(2)}) async-start(), calls=%async_computation.1 | async-start | bytes 524288 | tf_op jit(solution)/shard_map/psum | solution.py:102
  331.3 216.8 %copy-start.45 = (f32[256,256]{1,0:T(8,128)}, f32[256,256]{1,0:T(8,128)S(1)}, u32[]{:S(2)}) copy-start(f32[256,256]{1,0:T(8,128)S(1)} %fusion.88) | copy-start | bytes 786436
  444.8 558.4 %all-reduce.11.cloned.1.call-start = ((), (), s32[]{:S(2)}) async-start(), calls=%async_computation.2 | async-start | bytes 524288 | tf_op jit(solution)/shard_map/psum | solution.py:121
  557.7 4.9 copy-start.5
  573.6 295.0 %copy-start.14 = (bf16[256,1024]{1,0:T(8,128)(2,1)S(1)}, bf16[256,1024]{1,0:T(8,128)(2,1)}, u32[]{:S(2)}) copy-start(bf16[256,1024]{1,0:T(8,128)(2,1)} %get-tuple-element.61) | copy-start | bytes 1572868
  573.6 732.3 %all-reduce.13.cloned.1.call-start = ((), (), s32[]{:S(2)}) async-start(), calls=%async_computation.3 | async-start | bytes 786432 | tf_op jit(solution)/shard_map/psum | solution.py:139
  871.0 131.1 %copy-start.34 = (bf16[256,1024]{1,0:T(8,128)(2,1)S(1)}, bf16[256,1024]{1,0:T(8,128)(2,1)}, u32[]{:S(2)}) copy-start(bf16[256,1024]{1,0:T(8,128)(2,1)} %copy-done.33) | copy-start | bytes 1572868
  1030.9 4.1 copy-start.18
  1031.7 4.9 collective-permute-start.4
  1035.3 5.0 copy-start.35
  1035.3 5.0 collective-permute-start.5
  1040.6 6.0 copy-start.16
  1041.0 11.3 collective-permute-start.6
  1045.1 7.7 collective-permute-start.7
  1062.4 247.0 %copy-start.1 = (bf16[256,256]{1,0:T(8,128)(2,1)S(1)}, bf16[256,256]{1,0:T(8,128)(2,1)}, u32[]{:S(2)}) copy-start(bf16[256,256]{1,0:T(8,128)(2,1)} %param.10) | copy-start | bytes 393220
  (56 other events, 86.5 us)
Sparse Core Ops, SparseCore 0:
  329.3 115.5 all-reduce.6
  448.0 96.5 all-reduce.8
  573.8 212.6 all-reduce.10
  1052.5 253.4 all-reduce.12
